TPU v7x, 32 devices: a whole 2x2x4 slice. The times are simulated.
32 devices in a mesh: clips: 2 (over y), tm: 4 (over z), space: 4 (over x, core).
Axes of the slice: x: 2, y: 2, z: 4, core: 2. Of those that a mesh axis runs over, the one named last changes fastest.
Arguments:
- latent: bfloat16 [16, 8, 16, 16], P(('clips', 'tm'), 'space'), parts along dimension 0, may hold values from -6 to 6
- w_in: bfloat16 [3, 3, 3, 16, 384], replicated, may hold values from -0.3125 to 0.3125
- b_in: float32 [384], replicated, may hold values from -1.5 to 1.5
- gain_in: float32 [384], replicated, may hold values from 0.1 to 1.9
- w_time: bfloat16 [3, 384, 768], replicated, may hold values from -0.1875 to 0.1875
- b_time: float32 [768], replicated, may hold values from -1.5 to 1.5
- w_up: bfloat16 [3, 3, 384, 192], replicated, may hold values from -0.109375 to 0.109375
- b_up: float32 [192], replicated, may hold values from -1.5 to 1.5
Outputs:
- decoded: bfloat16 [32, 16, 32, 192], P(('clips', 'tm'), 'space'), parts along dimension 0
There are 2 independent parts, one for each index of `clips`. A program takes and returns all parts, laid end to end along the dimension named above; an argument that names none is the same for every part. Nothing has to cross between parts.
All inputs are finite; a program needn't handle non-finite values.
Results may differ from a plain program's by a relative error of at most 0.0055.
Values may be sent and summed in bfloat16 or wider, within the bound.
A program may use at most 64 MiB of HBM per device.

v0:
```python
import jax
import jax.numpy as jnp
from jax import lax
from jax.sharding import PartitionSpec as P

EPSILON = 1e-06


def with_halo(block, sides, width):
    for axis, dim in sides:
        count = lax.axis_size(axis)
        forward = [(i, i + 1) for i in range(count - 1)]
        backward = [(target, source) for source, target in forward]
        low = lax.ppermute(
            lax.slice_in_dim(block, block.shape[dim] - width, None, axis=dim), axis, forward
        )
        high = lax.ppermute(lax.slice_in_dim(block, 0, width, axis=dim), axis, backward)
        block = jnp.concatenate([low, block, high], axis=dim)
    return block


def passed_along(x, axis, by):
    count = lax.axis_size(axis)
    pairs = [(i, i + by) for i in range(count) if 0 <= i + by < count]
    return lax.ppermute(x, axis, pairs)


def margin_rows(joined):
    depth = 2
    return with_halo(joined, (("space", 1),), depth)


def entry_conv(extended, w_in, b_in, gain_in):
    frame_count = extended.shape[0] - 2
    row_count = extended.shape[1] - 2
    col_count = extended.shape[2]
    padded = jnp.pad(extended, ((0, 0), (0, 0), (1, 1), (0, 0)))
    tap_list = [
        padded[
            frame_tap : frame_tap + frame_count,
            row_tap : row_tap + row_count,
            col_tap : col_tap + col_count,
            :,
        ]
        for frame_tap in range(3)
        for row_tap in range(3)
        for col_tap in range(3)
    ]
    stacked = jnp.concatenate(tap_list, axis=3).reshape(frame_count * row_count * col_count, -1)
    hidden = (
        jnp.dot(stacked, w_in.reshape(stacked.shape[1], -1), preferred_element_type=jnp.float32)
        + b_in
    )
    inverse = lax.rsqrt(jnp.mean(hidden * hidden, axis=1, keepdims=True) + EPSILON)
    normed = jax.nn.silu(hidden * inverse * gain_in).astype(jnp.bfloat16)
    return normed.reshape(frame_count, row_count, col_count, -1)


def time_conv(extended, w_time, b_time):
    frame_count = extended.shape[0] - 2
    row_count = extended.shape[1]
    col_count = extended.shape[2]
    feature_width = extended.shape[3]
    tap_list = [extended[offset : offset + frame_count] for offset in range(3)]
    stacked = jnp.concatenate(tap_list, axis=3).reshape(
        frame_count * row_count * col_count, 3 * feature_width
    )
    result = (
        jnp.dot(stacked, w_time.reshape(3 * feature_width, -1), preferred_element_type=jnp.float32)
        + b_time
    )
    return result.astype(jnp.bfloat16).reshape(frame_count, row_count, col_count, -1)


def clear_outside(timed):
    row_total = timed.shape[1]
    position = lax.axis_index("space")
    space_count = lax.axis_size("space")
    row_ids = jnp.arange(row_total, dtype=jnp.int32)
    row_valid = ((row_ids > 0) | (position > 0)) & (
        (row_ids < row_total - 1) | (position < space_count - 1)
    )
    return jnp.where(row_valid[None, :, None, None], timed, jnp.zeros_like(timed))


def upsample_conv(timed, w_up, b_up):
    frame_count, row_total, col_count, double_width = timed.shape
    feature_width = double_width // 2
    halves = timed.reshape(frame_count, row_total, col_count, 2, feature_width)
    doubled = jnp.moveaxis(halves, 3, 1).reshape(
        2 * frame_count, row_total, col_count, feature_width
    )
    enlarged = jnp.repeat(jnp.repeat(doubled, 2, axis=1), 2, axis=2)[:, 1 : 2 * row_total - 1]
    padded = jnp.pad(enlarged, ((0, 0), (0, 0), (1, 1), (0, 0)))
    out_rows = 2 * row_total - 4
    out_cols = 2 * col_count
    tap_list = [
        padded[:, row_tap : row_tap + out_rows, col_tap : col_tap + out_cols, :]
        for row_tap in range(3)
        for col_tap in range(3)
    ]
    stacked = jnp.concatenate(tap_list, axis=3).reshape(
        2 * frame_count * out_rows * out_cols, 9 * feature_width
    )
    result = (
        jnp.dot(stacked, w_up.reshape(9 * feature_width, -1), preferred_element_type=jnp.float32)
        + b_up
    )
    return result.astype(jnp.bfloat16).reshape(2 * frame_count, out_rows, out_cols, -1)


def shards(latent, w_in, b_in, gain_in, w_time, b_time, w_up, b_up):
    earlier = passed_along(latent, "tm", 1)
    joined = jnp.concatenate([earlier, latent], axis=0)
    active = entry_conv(margin_rows(joined), w_in, b_in, gain_in)
    previous = passed_along(active, "tm", 1)
    context = jnp.concatenate([previous, active], axis=0)
    timed = clear_outside(time_conv(context, w_time, b_time))
    return upsample_conv(timed, w_up, b_up)


def solution(mesh):
    in_specs = (P(("clips", "tm"), "space", None, None), P(), P(), P(), P(), P(), P(), P())
    out_specs = P(("clips", "tm"), "space", None, None)
    return jax.shard_map(shards, mesh=mesh, in_specs=in_specs, out_specs=out_specs, check_vma=False)
```

profile of v0, /device:TPU:18, one launch (start us, length us, event | category | flops | bytes accessed | tf_op | source)
XLA Modules:
  0.0 33.7 jit_solution(15161917546235122889)
XLA Ops:
  0.0 0.0 copy-start
  0.0 3.6 %collective-permute-start = (bf16[2,2,16,16]{3,2,1,0:T(8,128)(2,1)}, bf16[2,2,16,16]{3,2,1,0:T(8,128)(2,1)S(1)}, u32[]{:S(2)}, u32[]{:S(2)}) collective-permute-start(bf16[2,2,16,16]{3,2,1,0:T(8,128)(2,1)} %param.8), channel_id=1, source_target_pairs={{0,4},{4,8},{8,12},{1,5},{5,9},{9,13},{2,6},{6,10},{10,14},{3,7},{... | collective-permute-start | bytes 6152 | tf_op jit(solution)/shard_map/ppermute | solution.py:25
  3.6 2.4 %collective-permute-done = bf16[2,2,16,16]{3,2,1,0:T(8,128)(2,1)S(1)} collective-permute-done((bf16[2,2,16,16]{3,2,1,0:T(8,128)(2,1)}, bf16[2,2,16,16]{3,2,1,0:T(8,128)(2,1)S(1)}, u32[]{:S(2)}, u32[]{:S(2)}) %collective-permute-start) | collective-permute-done | bytes 2080 | tf_op jit(solution)/shard_map/ppermute | solution.py:25
  6.0 0.6 %constant_dynamic-update-slice_fusion.1 = bf16[4,2,16,16]{3,2,1,0:T(8,128)(2,1)} fusion(bf16[2,2,16,16]{3,2,1,0:T(8,128)(2,1)S(1)} %collective-permute-done), kind=kLoop, calls=%fused_computation.64 | loop fusion | bytes 18432
  6.6 1.3 %constant_dynamic-update-slice_fusion = bf16[4,2,16,16]{3,2,1,0:T(8,128)(2,1)} fusion(bf16[4,2,16,16]{3,2,1,0:T(8,128)(2,1)} %constant_dynamic-update-slice_fusion.1, bf16[2,2,16,16]{3,2,1,0:T(8,128)(2,1)} %param.8), kind=kLoop, calls=%fused_computation.63 | loop fusion | bytes 32768 | tf_op jit(solution)/shard_map/concatenate | solution.py:114
  7.9 1.9 %collective-permute-start.1 = (bf16[4,2,16,16]{3,2,1,0:T(8,128)(2,1)}, bf16[4,2,16,16]{3,2,1,0:T(8,128)(2,1)}, u32[]{:S(2)}, u32[]{:S(2)}) collective-permute-start(bf16[4,2,16,16]{3,2,1,0:T(8,128)(2,1)} %constant_dynamic-update-slice_fusion), channel_id=1, source_target_pairs={{0,1},{1,2},{2,3},{4,5},{5,6},{6,7},{8,9},{9,10},{10,11},{12,13},{... | collective-permute-start | bytes 12296 | tf_op jit(solution)/shard_map/ppermute | solution.py:14
  9.8 3.6 %collective-permute-start.2 = (bf16[4,2,16,16]{3,2,1,0:T(8,128)(2,1)}, bf16[4,2,16,16]{3,2,1,0:T(8,128)(2,1)}, u32[]{:S(2)}, u32[]{:S(2)}) collective-permute-start(bf16[4,2,16,16]{3,2,1,0:T(8,128)(2,1)} %constant_dynamic-update-slice_fusion), channel_id=1, source_target_pairs={{1,0},{2,1},{3,2},{5,4},{6,5},{7,6},{9,8},{10,9},{11,10},{13,12},{... | collective-permute-start | bytes 12296 | tf_op jit(solution)/shard_map/ppermute | solution.py:17
  13.5 2.5 %copy.10 = bf16[3,3,384,192]{2,1,0,3:T(4,128)(2,1)S(1)} copy(bf16[3,3,384,192]{2,3,1,0:T(8,128)(2,1)} %param.14) | data formatting | bytes 2654208 | tf_op args[6]
  15.9 0.0 copy-start.2
  16.0 0.0 copy-start.3
  16.0 0.0 copy-start.4
  16.0 2.4 %reshape.69 = bf16[3456,192]{0,1:T(8,128)(2,1)} reshape(bf16[3,3,384,192]{2,1,0,3:T(4,128)(2,1)S(1)} %copy.10) | data formatting | bytes 2654208 | tf_op jit(solution)/shard_map/reshape | solution.py:106
  18.3 0.0 collective-permute-done.1
  18.3 0.0 collective-permute-done.2
  18.3 0.8 %pad_maximum_fusion.2 = bf16[4,6,16,16]{3,2,1,0:T(8,128)(2,1)S(1)} fusion(bf16[4,2,16,16]{3,2,1,0:T(8,128)(2,1)} %collective-permute-done.2, bf16[4,2,16,16]{3,2,1,0:T(8,128)(2,1)} %constant_dynamic-update-slice_fusion, bf16[4,2,16,16]{3,2,1,0:T(8,128)(2,1)} %collective-permute-done.1), kind=kLoop, calls=%fused_computation.48 | loop fusion | flops 12288 | bytes 24576 | tf_op jit(solution)/shard_map/concatenate | solution.py:18
  19.2 0.1 pad_slice_fusion.6
  19.3 1.0 %pad_maximum_fusion.3 = (bf16[2,4,16,16]{3,2,1,0:T(8,128)(2,1)S(1)}, bf16[2,4,16,16]{3,2,1,0:T(8,128)(2,1)S(1)}, bf16[2,4,16,16]{3,2,1,0:T(8,128)(2,1)S(1)}, bf1...) fusion(bf16[4,2,16,16]{3,2,1,0:T(8,128)(2,1)} %collective-permu, ...), kind=kLoop, calls=%fused_computation.61 | loop fusion | flops 49152 | bytes 176128 | tf_op jit(solution)/shard_map/concatenate | solution.py:18
  20.3 0.3 %concatenate.40 = bf16[2,4,16,432]{3,2,1,0:T(8,128)(2,1)S(1)} concatenate(bf16[2,4,16,16]{3,2,1,0:T(8,128)(2,1)S(1)} %get-tuple-element.39, bf16[2,4,16,16]{3,2,1,0:T(8,128)(2,1)S(1)} %get-tuple-element.35, bf16[2,4,16,16]{3,2,1,0:T(8,128)(2,1)S(1)} %get-tuple-element.8, bf16[2,4,16,16]{3,2,1,0:T(8,128)(2,1)S(1)} %get-tuple-element.9, ...), dimensions={3} | concatenate | bytes 221184 | tf_op jit(solution)/shard_map/concatenate | solution.py:49
  20.6 0.0 copy-done.2
  20.6 1.3 %multiply_reduce_fusion = (f32[128]{0:T(128)S(1)}, f32[128,384]{1,0:T(8,128)S(1)}) fusion(f32[384]{0:T(512)S(1)} %copy-done.2, bf16[128,432]{1,0:T(8,128)(2,1)S(1)} %bitcast.21, bf16[432,384]{1,0:T(8,128)(2,1)} %bitcast.24), kind=kOutput, calls=%fused_computation.45 | convolution fusion | flops 42614656 | bytes 641024 | tf_op jit(solution)/shard_map/dot_general | solution.py:51
  21.9 0.0 copy-done.3
  21.9 0.1 multiply_convert_fusion
  22.1 3.5 %collective-permute-start.3 = (bf16[2,4,16,384]{3,2,1,0:T(8,128)(2,1)S(1)}, bf16[2,4,16,384]{3,2,1,0:T(8,128)(2,1)S(1)}, u32[]{:S(2)}, u32[]{:S(2)}) collective-permute-start(bf16[2,4,16,384]{3,2,1,0:T(8,128)(2,1)S(1)} %bitcast.22), channel_id=1, source_target_pairs={{0,4},{4,8},{8,12},{1,5},{5,9},{9,13},{2,6},{6,10},{10,14},{3,7},{... | collective-permute-start | bytes 294920 | tf_op jit(solution)/shard_map/ppermute | solution.py:25
  25.6 3.0 %collective-permute-done.3 = bf16[2,4,16,384]{3,2,1,0:T(8,128)(2,1)S(1)} collective-permute-done((bf16[2,4,16,384]{3,2,1,0:T(8,128)(2,1)S(1)}, bf16[2,4,16,384]{3,2,1,0:T(8,128)(2,1)S(1)}, u32[]{:S(2)}, u32[]{:S(2)}) %collective-permute-start.3) | collective-permute-done | bytes 98336 | tf_op jit(solution)/shard_map/ppermute | solution.py:25
  28.6 0.0 copy-done
  28.6 0.0 copy-done.4
  28.6 0.4 %fusion = bf16[128,768]{1,0:T(8,128)(2,1)S(1)} fusion(bf16[1152,768]{1,0:T(8,128)(2,1)S(1)} %bitcast.18, bf16[128,384]{1,0:T(8,128)(2,1)S(1)} %multiply_convert_fusion, bf16[128,384]{1,0:T(8,128)(2,1)S(1)} %bitcast.27, bf16[128,384]{1,0:T(8,128)(2,1)S(1)} %bitcast.26, f32[768]{0:T(1024)S(1)} %copy-done.4), kind=kOutput, calls=%fused_computation.2 | convolution fusion | flops 227573760 | bytes 2264064 | tf_op jit(solution)/shard_map/dot_general | solution.py:69
  29.1 0.1 broadcast_select_fusion
  29.3 0.5 %broadcast_in_dim.26 = bf16[4,8,16,2,384]{4,3,2,1,0:T(2,128)(2,1)S(1)} broadcast(bf16[4,8,16,384]{3,2,1,0:T(8,128)(2,1)S(1)} %bitcast.19), dimensions={0,1,2,4} | broadcast | bytes 1179648 | tf_op jit(solution)/shard_map/broadcast_in_dim | solution.py:93
  29.7 0.3 reshape.67
  30.0 0.1 slice.194
  30.1 0.1 fusion.2
  30.2 0.0 copy-start.1
  30.2 0.0 copy-start.5
  30.2 0.1 slice_dynamic-update-slice_fusion.2
  30.3 0.1 fusion.3
  30.4 0.1 fusion.4
  30.6 0.1 slice_dynamic-update-slice_fusion.1
  30.7 0.1 fusion.5
  30.8 0.1 fusion.6
  31.0 0.1 slice_dynamic-update-slice_fusion
  31.0 0.1 fusion.7
  31.2 0.4 %copy-done.1 = bf16[3456,192]{0,1:T(8,128)(2,1)S(1)} copy-done((bf16[3456,192]{0,1:T(8,128)(2,1)S(1)}, bf16[3456,192]{0,1:T(8,128)(2,1)}, u32[]{:S(2)}) %copy-start.1) | copy-done | bytes 1327128
  31.5 0.0 copy-done.5
  31.5 1.3 %fusion.1 = bf16[512,192]{0,1:T(8,128)(2,1)S(1)} fusion(bf16[512,3456]{1,0:T(8,128)(2,1)S(1)} %bitcast.28, bf16[3456,192]{0,1:T(8,128)(2,1)S(1)} %copy-done.1, f32[192]{0:T(256)S(1)} %copy-done.5), kind=kOutput, calls=%fused_computation.3 | convolution fusion | flops 679673856 | bytes 5063424 | tf_op jit(solution)/shard_map/dot_general | solution.py:106
  32.9 0.8 %copy.11 = bf16[512,192]{1,0:T(8,128)(2,1)} copy(bf16[512,192]{0,1:T(8,128)(2,1)S(1)} %fusion.1) | data formatting | bytes 393216 | tf_op jit(solution)/shard_map/convert_element_type | solution.py:109
  (6 shorter events, 0.1 us)
Async XLA Ops:
  0.0 28.6 %copy-start = (bf16[3,384,768]{2,1,0:T(8,128)(2,1)S(1)}, bf16[3,384,768]{2,1,0:T(8,128)(2,1)}, u32[]{:S(2)}) copy-start(bf16[3,384,768]{2,1,0:T(8,128)(2,1)} %param.12) | copy-start | bytes 5308420
  0.0 6.0 %collective-permute-start = (bf16[2,2,16,16]{3,2,1,0:T(8,128)(2,1)}, bf16[2,2,16,16]{3,2,1,0:T(8,128)(2,1)S(1)}, u32[]{:S(2)}, u32[]{:S(2)}) collective-permute-start(bf16[2,2,16,16]{3,2,1,0:T(8,128)(2,1)} %param.8), channel_id=1, source_target_pairs={{0,4},{4,8},{8,12},{1,5},{5,9},{9,13},{2,6},{6,10},{10,14},{3,7},{... | collective-permute-start | bytes 6152 | tf_op jit(solution)/shard_map/ppermute | solution.py:25
  7.9 10.4 %collective-permute-start.1 = (bf16[4,2,16,16]{3,2,1,0:T(8,128)(2,1)}, bf16[4,2,16,16]{3,2,1,0:T(8,128)(2,1)}, u32[]{:S(2)}, u32[]{:S(2)}) collective-permute-start(bf16[4,2,16,16]{3,2,1,0:T(8,128)(2,1)} %constant_dynamic-update-slice_fusion), channel_id=1, source_target_pairs={{0,1},{1,2},{2,3},{4,5},{5,6},{6,7},{8,9},{9,10},{10,11},{12,13},{... | collective-permute-start | bytes 12296 | tf_op jit(solution)/shard_map/ppermute | solution.py:14
  9.8 8.5 %collective-permute-start.2 = (bf16[4,2,16,16]{3,2,1,0:T(8,128)(2,1)}, bf16[4,2,16,16]{3,2,1,0:T(8,128)(2,1)}, u32[]{:S(2)}, u32[]{:S(2)}) collective-permute-start(bf16[4,2,16,16]{3,2,1,0:T(8,128)(2,1)} %constant_dynamic-update-slice_fusion), channel_id=1, source_target_pairs={{1,0},{2,1},{3,2},{5,4},{6,5},{7,6},{9,8},{10,9},{11,10},{13,12},{... | collective-permute-start | bytes 12296 | tf_op jit(solution)/shard_map/ppermute | solution.py:17
  15.9 4.7 %copy-start.2 = (f32[384]{0:T(512)S(1)}, f32[384]{0:T(512)}, u32[]{:S(2)}) copy-start(f32[384]{0:T(512)} %param.10) | copy-start | bytes 4612
  16.0 6.0 %copy-start.3 = (f32[384]{0:T(512)S(1)}, f32[384]{0:T(512)}, u32[]{:S(2)}) copy-start(f32[384]{0:T(512)} %param.11) | copy-start | bytes 4612
  16.0 12.6 %copy-start.4 = (f32[768]{0:T(1024)S(1)}, f32[768]{0:T(1024)}, u32[]{:S(2)}) copy-start(f32[768]{0:T(1024)} %param.13) | copy-start | bytes 9220
  22.1 6.5 %collective-permute-start.3 = (bf16[2,4,16,384]{3,2,1,0:T(8,128)(2,1)S(1)}, bf16[2,4,16,384]{3,2,1,0:T(8,128)(2,1)S(1)}, u32[]{:S(2)}, u32[]{:S(2)}) collective-permute-start(bf16[2,4,16,384]{3,2,1,0:T(8,128)(2,1)S(1)} %bitcast.22), channel_id=1, source_target_pairs={{0,4},{4,8},{8,12},{1,5},{5,9},{9,13},{2,6},{6,10},{10,14},{3,7},{... | collective-permute-start | bytes 294920 | tf_op jit(solution)/shard_map/ppermute | solution.py:25
  30.2 1.3 %copy-start.1 = (bf16[3456,192]{0,1:T(8,128)(2,1)S(1)}, bf16[3456,192]{0,1:T(8,128)(2,1)}, u32[]{:S(2)}) copy-start(bf16[3456,192]{0,1:T(8,128)(2,1)} %reshape.69) | copy-start | bytes 3981316
  30.2 1.3 %copy-start.5 = (f32[192]{0:T(256)S(1)}, f32[192]{0:T(256)}, u32[]{:S(2)}) copy-start(f32[192]{0:T(256)} %param.15) | copy-start | bytes 2308
where the time goes:
time: 34.2 us; the launch traced here: 33.7 us
  starting transfers between devices  12.6 us (37%)
  local copies, waits for them, and re-layouts  10.3 us (30%)
  waiting for transfers between devices  5.36 us (16%)
  matrix products  3.02 us (9%)
  other arithmetic  2.06 us (6%)
    ppermute x2, starting transfers between devices, passed_along(): return lax.ppermute(x, axis, pairs)  7.09 us
    ppermute x2, waiting for transfers between devices, passed_along(): return lax.ppermute(x, axis, pairs)  5.35 us
    unnamed x22, local copies, waits for them, and re-layouts  4.32 us
    ppermute x1, starting transfers between devices, with_halo(): lax.ppermute(lax.slice_in_dim(block, 0, width, axis=dim), axis, backward)  3.64 us
    reshape x1, local copies, waits for them, and re-layouts, upsample_conv(): w_up.reshape(9 * feature_width, -1)  2.36 us
    ppermute x1, starting transfers between devices, with_halo(): lax.ppermute(lax.slice_in_dim(block, block.shape[dim] - width, None, axis...  1.91 us
    concatenate x2, other arithmetic, with_halo(): block = jnp.concatenate([low, block, high], axis=dim)  1.78 us
    concatenate x1, local copies, waits for them, and re-layouts, shards(): joined = jnp.concatenate([earlier, latent], axis=0)  1.32 us
  transfers between devices with their start and end apart: 4, of which 2 were waited for; matrix products, arithmetic and copies ran while one was open for 14% of the time, Pallas kernels for 0%

commit v1 on v0

v1 whole, which is shorter than its diff:
```python
import functools

import jax
import jax.numpy as jnp
from jax import lax
from jax.experimental import pallas as pl
from jax.experimental.pallas import tpu as pltpu
from jax.sharding import PartitionSpec as P

EPSILON = 1e-06
MESH = pl.DeviceIdType.MESH
LANES = 128


def tap_groups(phase):
    return [(-1, (0,)), (0, (1, 2))] if phase == 0 else [(0, (0, 1)), (1, (2,))]


def kernel(
    sizes,
    lat_hbm,
    w_in_hbm,
    b_in_hbm,
    gain_hbm,
    w_time_hbm,
    b_time_hbm,
    w_up_hbm,
    b_up_hbm,
    out_hbm,
    lat_v,
    ext,
    taps,
    w_in_v,
    w_time_v,
    w_up_v,
    w_phase,
    b_in_v,
    gain_v,
    b_time_v,
    b_up_v,
    active,
    summed,
    shifted,
    wide,
    out_v,
    local_sem,
    w_in_sem,
    out_sem,
    send_sem,
    recv_sem,
):
    tm_count, space_count, reach, frames, rows, cols, zc = sizes
    ch = w_time_v.shape[1]
    co = w_up_v.shape[2]
    halo = 1
    own_rows = rows
    out_rows = rows + 2
    tm = lax.axis_index("tm")
    space = lax.axis_index("space")
    offsets = [(d, o) for d in range(reach, -1, -1) for o in (-1, 1, 0) if (d, o) != (0, 0)]

    def inside(d, o):
        t, s = tm + d, space + o
        return (t >= 0) & (t < tm_count) & (s >= 0) & (s < space_count)

    barrier = pltpu.get_barrier_semaphore()
    for d, o in offsets:

        @pl.when(inside(-d, -o))
        def _():
            pl.semaphore_signal(
                barrier, inc=1, device_id={"tm": tm - d, "space": space - o}, device_id_type=MESH
            )

    lat_copy = pltpu.make_async_copy(lat_hbm, lat_v, local_sem.at[0])
    lat_copy.start()
    w_in_copies = [
        pltpu.make_async_copy(w_in_hbm.at[:, b, e], w_in_v.at[:, e, b], w_in_sem.at[3 * b + e])
        for b in range(3)
        for e in range(3)
    ]
    up_copy = pltpu.make_async_copy(w_up_hbm, w_up_v, local_sem.at[1])
    time_copy = pltpu.make_async_copy(w_time_hbm, w_time_v, local_sem.at[2])
    small_copies = [
        pltpu.make_async_copy(src, dst, local_sem.at[3 + i])
        for i, (src, dst) in enumerate(
            ((b_in_hbm, b_in_v), (gain_hbm, gain_v), (b_time_hbm, b_time_v), (b_up_hbm, b_up_v))
        )
    ]
    for copy in [up_copy] + w_in_copies + small_copies + [time_copy]:
        copy.start()

    for d, o in offsets:

        @pl.when(jnp.logical_not(inside(-d, -o)))
        def _():
            ext[reach - d, halo - o] = jnp.zeros(ext.shape[2:], ext.dtype)

    w_in_v[:, :, 3] = jnp.zeros((3, 3) + w_in_v.shape[3:], w_in_v.dtype)

    lat_copy.wait()
    own = lat_v[...].astype(jnp.float32)
    pieces = [own[f, r] for f in range(frames) for r in range(rows)]
    pieces.append(jnp.zeros((cols, LANES - frames * rows * zc), jnp.float32))
    ext[reach, halo] = jnp.concatenate(pieces, axis=1).astype(ext.dtype)

    expected = sum(inside(d, o).astype(jnp.int32) for d, o in offsets)
    pl.semaphore_wait(barrier, expected)

    def remote(d, o):
        slot = (reach - d) * 3 + (halo - o)
        return pltpu.make_async_remote_copy(
            src_ref=ext.at[reach, halo],
            dst_ref=ext.at[reach - d, halo - o],
            send_sem=send_sem.at[slot],
            recv_sem=recv_sem.at[slot],
            device_id={"tm": tm + d, "space": space + o},
            device_id_type=MESH,
        )

    for d, o in offsets:

        @pl.when(inside(d, o))
        def _():
            remote(d, o).start()

    up_copy.wait()
    step = 16

    @pl.loop(0, co // step)
    def _(i):
        at = pl.multiple_of(i * step, step)
        w = [
            [w_up_v[b, e, pl.ds(at, step), :].astype(jnp.float32) for e in range(3)]
            for b in range(3)
        ]
        for q in range(2):
            for m, (_, es) in enumerate(tap_groups(q)):
                col = [sum(w[b][e] for e in es[1:]) + w[b][es[0]] if len(es) > 1 else w[b][es[0]] for b in range(3)]
                for p in range(2):
                    for n, (_, bs) in enumerate(tap_groups(p)):
                        both = col[bs[0]] + col[bs[1]] if len(bs) > 1 else col[bs[0]]
                        place = pl.ds((2 * n + m) * ch, ch)
                        w_phase[p, q, pl.ds(at, step), place] = both.astype(w_phase.dtype)

    for copy in w_in_copies + small_copies:
        copy.wait()

    def arrived(d, o):
        @pl.when(inside(-d, -o))
        def _():
            remote(d, o).wait_recv()

    lane = lax.broadcasted_iota(jnp.int32, (1, LANES), 1)
    col_id = lax.broadcasted_iota(jnp.int32, (out_rows * cols, 1), 0) % cols

    def gather_taps(first, last):
        for frame in range(first, last):
            j, f = divmod(frame, frames)
            base = f * rows * zc
            line = jnp.concatenate(
                [
                    ext[j, k].astype(jnp.float32)[:, base : base + rows * zc]
                    for k in range(3)
                ]
                + [jnp.zeros((cols, LANES - 3 * rows * zc), jnp.float32)],
                axis=1,
            )
            start = rows - 2
            turned = [
                pltpu.roll(line, (LANES - (start + q) * zc) % LANES, 1) if start + q else line
                for q in range(out_rows)
            ]
            mid = jnp.concatenate(turned, axis=0)
            mid = jnp.where(lane < 3 * zc, mid, 0.0)
            left = jnp.where(col_id == 0, 0.0, pltpu.roll(mid, 1, 0))
            right = jnp.where(col_id == cols - 1, 0.0, pltpu.roll(mid, out_rows * cols - 1, 0))
            pair = left + pltpu.roll(mid, 4 * zc, 1)
            taps[frame] = jnp.concatenate([pair, right[:, : 4 * zc]], axis=1).astype(taps.dtype)

    def entry(first, count):
        total = None
        for a in range(3):
            lhs = taps[pl.ds(first + a, count)].reshape(count * out_rows * cols, -1)
            term = jnp.dot(lhs, w_in_v[a].reshape(12 * zc, ch), preferred_element_type=jnp.float32)
            total = term if total is None else total + term
        hidden = total + b_in_v[...].reshape(1, ch)
        inverse = lax.rsqrt(jnp.mean(hidden * hidden, axis=1, keepdims=True) + EPSILON)
        v = hidden * inverse * gain_v[...].reshape(1, ch)
        return (v / (1.0 + jnp.exp(-v))).astype(active.dtype).reshape(count, out_rows * cols, ch)

    head = reach * frames - 4
    for d, o in offsets:
        if d * frames <= frames + 1:
            arrived(d, o)
    gather_taps(head + 2, head + 4 + frames)
    active[pl.ds(2, frames)] = entry(head + 2, frames)
    time_copy.wait()
    size = out_rows * cols

    def times(first, count, tap):
        lhs = active[pl.ds(first, count)].reshape(count * size, ch)
        return jnp.dot(lhs, w_time_v[tap], preferred_element_type=jnp.float32)

    summed[...] = times(2, frames, 2) + b_time_v[...].reshape(1, 2 * ch)
    for tap in range(2):
        skip = 2 - tap
        if frames > skip:
            summed[skip * size :] = summed[skip * size :] + times(2, frames - skip, tap)

    for d, o in offsets:
        if d * frames > frames + 1:
            arrived(d, o)
    gather_taps(head, head + 2)
    early = entry(head, 2)
    known = lax.broadcasted_iota(jnp.int32, (2, 1, 1), 0) + (tm * frames - 2) >= 0
    active[pl.ds(0, 2)] = jnp.where(known, early, jnp.zeros_like(early))
    for tap in range(2):
        n = min(2 - tap, frames)
        summed[: n * size] = summed[: n * size] + times(tap, n, tap)

    row_id = lax.broadcasted_iota(jnp.int32, (frames * size, 1), 0) % size // cols
    column = lax.broadcasted_iota(jnp.int32, (frames * size, 1), 0) % cols
    row_ok = ((row_id > 0) | (space > 0)) & ((row_id < out_rows - 1) | (space < space_count - 1))
    for half in range(2):
        part = summed[:, half * ch : (half + 1) * ch].astype(shifted.dtype).astype(jnp.float32)
        part = jnp.where(row_ok, part, 0.0)
        back = jnp.where(column == 0, 0.0, pltpu.roll(part, 1, 0))
        ahead = jnp.where(column == cols - 1, 0.0, pltpu.roll(part, frames * size - 1, 0))
        for i, moved in enumerate((back, part, ahead)):
            shifted[i, :, half] = moved.astype(shifted.dtype).reshape(frames, out_rows, cols, ch)

    out_copies = []
    for p in range(2):
        for q in range(2):
            lhs = jnp.concatenate(
                [
                    shifted[1 + dc, :, :, pl.ds(1 + dr, own_rows)].reshape(
                        2 * frames * own_rows * cols, ch
                    )
                    for dr, _ in tap_groups(p)
                    for dc, _ in tap_groups(q)
                ],
                axis=1,
            )
            y = lax.dot_general(
                lhs, w_phase[p, q], (((1,), (1,)), ((), ())), preferred_element_type=jnp.float32
            )
            y = y + b_up_v[...].reshape(1, co)
            y = y.reshape(2 * frames, own_rows, cols, co)
            for g in range(2 * frames):
                for r in range(own_rows):
                    part = y[g, r]
                    low = part[:, :LANES]
                    wide[0, g, 2 * r + p, pl.ds(q, cols, stride=2), :] = low
                    rest = jnp.concatenate(
                        [part[:, LANES:], jnp.zeros((cols, 2 * LANES - co), jnp.float32)], axis=1
                    )
                    wide[1, g, 2 * r + p, pl.ds(q, cols, stride=2), :] = rest
        for r in range(own_rows):
            row = 2 * r + p
            out_v[:, row, :, :LANES] = wide[0, :, row].astype(out_v.dtype)
            out_v[:, row, :, LANES:] = wide[1, :, row][:, :, : co - LANES].astype(out_v.dtype)
            copy = pltpu.make_async_copy(out_v.at[:, row], out_hbm.at[:, row], out_sem.at[row])
            copy.start()
            out_copies.append(copy)

    for d, o in offsets:

        @pl.when(inside(d, o))
        def _():
            remote(d, o).wait_send()

    for copy in out_copies:
        copy.wait()


def shards(tm_count, space_count, latent, w_in, b_in, gain_in, w_time, b_time, w_up, b_up):
    frames, rows, cols, zc = latent.shape
    ch, co = w_in.shape[-1], w_up.shape[-1]
    reach = -(-4 // frames)
    out_rows = rows + 2
    size = out_rows * cols
    bf16, f32 = jnp.bfloat16, jnp.float32
    any_spec = pl.BlockSpec(memory_space=pl.ANY)
    return pl.pallas_call(
        functools.partial(kernel, (tm_count, space_count, reach, frames, rows, cols, zc)),
        out_shape=jax.ShapeDtypeStruct((2 * frames, 2 * rows, 2 * cols, co), bf16),
        in_specs=[any_spec] * 8,
        out_specs=any_spec,
        scratch_shapes=[
            pltpu.VMEM(latent.shape, bf16),
            pltpu.VMEM((reach + 1, 3, cols, LANES), bf16),
            pltpu.VMEM(((reach + 1) * frames, size, 12 * zc), bf16),
            pltpu.VMEM((3, 3, 4, zc, ch), bf16),
            pltpu.VMEM(w_time.shape, bf16),
            pltpu.VMEM((3, 3, co, ch), bf16),
            pltpu.VMEM((2, 2, co, 4 * ch), bf16),
            pltpu.VMEM((ch,), f32),
            pltpu.VMEM((ch,), f32),
            pltpu.VMEM((2 * ch,), f32),
            pltpu.VMEM((co,), f32),
            pltpu.VMEM((frames + 2, size, ch), bf16),
            pltpu.VMEM((frames * size, 2 * ch), f32),
            pltpu.VMEM((3, frames, 2, out_rows, cols, ch), bf16),
            pltpu.VMEM((2, 2 * frames, 2 * rows, 2 * cols, LANES), f32),
            pltpu.VMEM((2 * frames, 2 * rows, 2 * cols, co), bf16),
            pltpu.SemaphoreType.DMA((7,)),
            pltpu.SemaphoreType.DMA((9,)),
            pltpu.SemaphoreType.DMA((2 * rows,)),
            pltpu.SemaphoreType.DMA(((reach + 1) * 3,)),
            pltpu.SemaphoreType.DMA(((reach + 1) * 3,)),
        ],
        compiler_params=pltpu.CompilerParams(collective_id=0, has_side_effects=True),
    )(
        latent,
        w_in,
        b_in,
        gain_in,
        w_time,
        b_time,
        jnp.swapaxes(w_up, 2, 3),
        b_up,
    )


def solution(mesh):
    in_specs = (P(("clips", "tm"), "space", None, None), P(), P(), P(), P(), P(), P(), P())
    out_specs = P(("clips", "tm"), "space", None, None)
    body = functools.partial(shards, mesh.shape["tm"], mesh.shape["space"])
    return jax.shard_map(body, mesh=mesh, in_specs=in_specs, out_specs=out_specs, check_vma=False)
```

time: 34.2 us -> 12.1 us (0.35)
  the two profiles are of different devices: /device:TPU:18 before, /device:TPU:1 now
where the time goes in v1:
time: 12.1 us; the launch traced here: 11.9 us
  Pallas kernels  10.3 us (85%)
  local copies, waits for them, and re-layouts  1.67 us (14%)
    pallas_call x1, Pallas kernels, shards(): pl.pallas_call(functools.partial(kernel, (tm_count, space_count, reach, f...  10.3 us
    unnamed x1, local copies, waits for them, and re-layouts  1.67 us

profile of v1, /device:TPU:1, one launch (start us, length us, event | category | flops | bytes accessed | tf_op | source)
XLA Modules:
  0.0 11.9 jit_solution(7392943634170221607)
XLA Ops:
  0.0 10.3 %shard_map.82 = bf16[4,4,32,192]{3,2,1,0:T(8,128)(2,1)} custom-call(bf16[2,2,16,16]{3,2,1,0:T(8,128)(2,1)} %lat_hbm.1, bf16[3,3,3,16,384]{4,3,2,1,0:T(8,128)(2,1)} %w_in_hbm.1, f32[384]{0:T(512)} %b_in_hbm.1, f32[384]{0:T(512)} %gain_hbm.1, bf16[3,384,768]{2,1,0:T(8,128)(2,1)} %w_time_hbm.1, f32[768]{0:T(1024)} %b_time_hbm.1, ...), custom_call_target="tpu_custom_call" | custom-call | tf_op jit(solution)/shard_map/pallas_call | solution.py:286
  10.3 1.7 %copy.10 = bf16[4,4,32,192]{3,2,1,0:T(8,128)(2,1)} copy(bf16[4,4,32,192]{3,2,1,0:T(8,128)(2,1)} %shard_map.82) | data formatting | bytes 393216

commit v2 on v1

--- a/solution.py
+++ b/solution.py
@@ -10,6 +10,7 @@
 EPSILON = 1e-06
 MESH = pl.DeviceIdType.MESH
 LANES = 128
+VMEM_BYTES = 67043328
 
 
 def tap_groups(phase):
@@ -26,7 +27,7 @@
     b_time_hbm,
     w_up_hbm,
     b_up_hbm,
-    out_hbm,
+    out_v,
     lat_v,
     ext,
     taps,
@@ -42,10 +43,8 @@
     summed,
     shifted,
     wide,
-    out_v,
     local_sem,
     w_in_sem,
-    out_sem,
     send_sem,
     recv_sem,
 ):
@@ -230,7 +229,6 @@
         for i, moved in enumerate((back, part, ahead)):
             shifted[i, :, half] = moved.astype(shifted.dtype).reshape(frames, out_rows, cols, ch)
 
-    out_copies = []
     for p in range(2):
         for q in range(2):
             lhs = jnp.concatenate(
@@ -261,18 +259,12 @@
             row = 2 * r + p
             out_v[:, row, :, :LANES] = wide[0, :, row].astype(out_v.dtype)
             out_v[:, row, :, LANES:] = wide[1, :, row][:, :, : co - LANES].astype(out_v.dtype)
-            copy = pltpu.make_async_copy(out_v.at[:, row], out_hbm.at[:, row], out_sem.at[row])
-            copy.start()
-            out_copies.append(copy)
 
     for d, o in offsets:
 
         @pl.when(inside(d, o))
         def _():
             remote(d, o).wait_send()
-
-    for copy in out_copies:
-        copy.wait()
 
 
 def shards(tm_count, space_count, latent, w_in, b_in, gain_in, w_time, b_time, w_up, b_up):
@@ -285,9 +277,9 @@
     any_spec = pl.BlockSpec(memory_space=pl.ANY)
     return pl.pallas_call(
         functools.partial(kernel, (tm_count, space_count, reach, frames, rows, cols, zc)),
-        out_shape=jax.ShapeDtypeStruct((2 * frames, 2 * rows, 2 * cols, co), bf16),
+        out_shape=pltpu.VMEM((2 * frames, 2 * rows, 2 * cols, co), bf16),
         in_specs=[any_spec] * 8,
-        out_specs=any_spec,
+        out_specs=pl.BlockSpec(memory_space=pltpu.VMEM),
         scratch_shapes=[
             pltpu.VMEM(latent.shape, bf16),
             pltpu.VMEM((reach + 1, 3, cols, LANES), bf16),
@@ -304,14 +296,12 @@
             pltpu.VMEM((frames * size, 2 * ch), f32),
             pltpu.VMEM((3, frames, 2, out_rows, cols, ch), bf16),
             pltpu.VMEM((2, 2 * frames, 2 * rows, 2 * cols, LANES), f32),
-            pltpu.VMEM((2 * frames, 2 * rows, 2 * cols, co), bf16),
             pltpu.SemaphoreType.DMA((7,)),
             pltpu.SemaphoreType.DMA((9,)),
-            pltpu.SemaphoreType.DMA((2 * rows,)),
             pltpu.SemaphoreType.DMA(((reach + 1) * 3,)),
             pltpu.SemaphoreType.DMA(((reach + 1) * 3,)),
         ],
-        compiler_params=pltpu.CompilerParams(collective_id=0, has_side_effects=True),
+        compiler_params=pltpu.CompilerParams(collective_id=0, has_side_effects=True, vmem_limit_bytes=VMEM_BYTES - 2 * frames * 2 * rows * 2 * cols * (-(-co // LANES) * LANES) * 2),
     )(
         latent,
         w_in,

time: 12.1 us -> 10.4 us (0.86)
  local copies, waits for them, and re-layouts: 1.67 us -> 0.71 us
  Pallas kernels: 10.3 us -> 9.58 us
    unnamed x1, local copies, waits for them, and re-layouts: 1.67 us -> 0.71 us
    pallas_call x1, Pallas kernels: 10.3 us -> 9.58 us  [shards(): pl.pallas_call(functools.partial(kernel, (tm_count, space_count, reach, f...]
where the time goes in v2:
time: 10.4 us; the launch traced here: 10.3 us
  Pallas kernels  9.58 us (92%)
  local copies, waits for them, and re-layouts  0.71 us (7%)
    pallas_call x1, Pallas kernels, shards(): pl.pallas_call(functools.partial(kernel, (tm_count, space_count, reach, f...  9.58 us
    unnamed x1, local copies, waits for them, and re-layouts  0.71 us

profile of v2, /device:TPU:1, one launch (start us, length us, event | category | flops | bytes accessed | tf_op | source)
XLA Modules:
  0.0 10.3 jit_solution(2505204834183706385)
XLA Ops:
  0.0 9.6 %shard_map.82 = bf16[4,4,32,192]{3,2,1,0:T(8,128)(2,1)S(1)} custom-call(bf16[2,2,16,16]{3,2,1,0:T(8,128)(2,1)} %lat_hbm.1, bf16[3,3,3,16,384]{4,3,2,1,0:T(8,128)(2,1)} %w_in_hbm.1, f32[384]{0:T(512)} %b_in_hbm.1, f32[384]{0:T(512)} %gain_hbm.1, bf16[3,384,768]{2,1,0:T(8,128)(2,1)} %w_time_hbm.1, f32[768]{0:T(1024)} %b_time_hbm.1, ...), custom_call_target="tpu_custom_call" | custom-call | tf_op jit(solution)/shard_map/pallas_call | solution.py:278
  9.6 0.7 %copy.10 = bf16[4,4,32,192]{3,2,1,0:T(8,128)(2,1)} copy(bf16[4,4,32,192]{3,2,1,0:T(8,128)(2,1)S(1)} %shard_map.82) | data formatting | bytes 393216

commit v3 on v2

--- a/solution.py
+++ b/solution.py
@@ -56,20 +56,19 @@
     out_rows = rows + 2
     tm = lax.axis_index("tm")
     space = lax.axis_index("space")
-    offsets = [(d, o) for d in range(reach, -1, -1) for o in (-1, 1, 0) if (d, o) != (0, 0)]
-
-    def inside(d, o):
-        t, s = tm + d, space + o
-        return (t >= 0) & (t < tm_count) & (s >= 0) & (s < space_count)
+    low, high = space > 0, space < space_count - 1
+    later = tm < tm_count - 1
 
     barrier = pltpu.get_barrier_semaphore()
-    for d, o in offsets:
-
-        @pl.when(inside(-d, -o))
-        def _():
-            pl.semaphore_signal(
-                barrier, inc=1, device_id={"tm": tm - d, "space": space - o}, device_id_type=MESH
-            )
+    for there, target in (
+        (low, {"space": space - 1}),
+        (high, {"space": space + 1}),
+        (tm > 0, {"tm": tm - 1}),
+    ):
+
+        @pl.when(there)
+        def _():
+            pl.semaphore_signal(barrier, inc=1, device_id=target, device_id_type=MESH)
 
     lat_copy = pltpu.make_async_copy(lat_hbm, lat_v, local_sem.at[0])
     lat_copy.start()
@@ -89,11 +88,17 @@
     for copy in [up_copy] + w_in_copies + small_copies + [time_copy]:
         copy.start()
 
-    for d, o in offsets:
-
-        @pl.when(jnp.logical_not(inside(-d, -o)))
-        def _():
-            ext[reach - d, halo - o] = jnp.zeros(ext.shape[2:], ext.dtype)
+    for there, k in ((low, 0), (high, 2)):
+
+        @pl.when(jnp.logical_not(there))
+        def _():
+            ext[reach, k] = jnp.zeros(ext.shape[2:], ext.dtype)
+
+    for h in range(1, reach + 1):
+
+        @pl.when(tm < h)
+        def _():
+            ext[reach - h] = jnp.zeros(ext.shape[1:], ext.dtype)
 
     w_in_v[:, :, 3] = jnp.zeros((3, 3) + w_in_v.shape[3:], w_in_v.dtype)
 
@@ -103,25 +108,35 @@
     pieces.append(jnp.zeros((cols, LANES - frames * rows * zc), jnp.float32))
     ext[reach, halo] = jnp.concatenate(pieces, axis=1).astype(ext.dtype)
 
-    expected = sum(inside(d, o).astype(jnp.int32) for d, o in offsets)
-    pl.semaphore_wait(barrier, expected)
-
-    def remote(d, o):
-        slot = (reach - d) * 3 + (halo - o)
+    pl.semaphore_wait(
+        barrier, low.astype(jnp.int32) + high.astype(jnp.int32) + later.astype(jnp.int32)
+    )
+
+    def along_rows(o):
         return pltpu.make_async_remote_copy(
             src_ref=ext.at[reach, halo],
-            dst_ref=ext.at[reach - d, halo - o],
-            send_sem=send_sem.at[slot],
-            recv_sem=recv_sem.at[slot],
-            device_id={"tm": tm + d, "space": space + o},
+            dst_ref=ext.at[reach, halo - o],
+            send_sem=send_sem.at[reach + (o + 1) // 2],
+            recv_sem=recv_sem.at[reach + (o + 1) // 2],
+            device_id={"space": space + o},
             device_id_type=MESH,
         )
 
-    for d, o in offsets:
-
-        @pl.when(inside(d, o))
-        def _():
-            remote(d, o).start()
+    def along_time(h):
+        return pltpu.make_async_remote_copy(
+            src_ref=ext.at[reach - h + 1],
+            dst_ref=ext.at[reach - h],
+            send_sem=send_sem.at[h - 1],
+            recv_sem=recv_sem.at[h - 1],
+            device_id={"tm": tm + 1},
+            device_id_type=MESH,
+        )
+
+    for there, o in ((low, -1), (high, 1)):
+
+        @pl.when(there)
+        def _():
+            along_rows(o).start()
 
     up_copy.wait()
     step = 16
@@ -142,13 +157,25 @@
                         place = pl.ds((2 * n + m) * ch, ch)
                         w_phase[p, q, pl.ds(at, step), place] = both.astype(w_phase.dtype)
 
+    for there, o in ((low, 1), (high, -1)):
+
+        @pl.when(there)
+        def _():
+            along_rows(o).wait_recv()
+
+    def pass_on(h):
+        @pl.when(later & (tm >= h - 1))
+        def _():
+            along_time(h).start()
+
+    def arrived(h):
+        @pl.when(tm >= h)
+        def _():
+            along_time(h).wait_recv()
+
+    pass_on(1)
     for copy in w_in_copies + small_copies:
         copy.wait()
-
-    def arrived(d, o):
-        @pl.when(inside(-d, -o))
-        def _():
-            remote(d, o).wait_recv()
 
     lane = lax.broadcasted_iota(jnp.int32, (1, LANES), 1)
     col_id = lax.broadcasted_iota(jnp.int32, (out_rows * cols, 1), 0) % cols
@@ -189,9 +216,11 @@
         return (v / (1.0 + jnp.exp(-v))).astype(active.dtype).reshape(count, out_rows * cols, ch)
 
     head = reach * frames - 4
-    for d, o in offsets:
-        if d * frames <= frames + 1:
-            arrived(d, o)
+    near = -(-2 // frames)
+    for h in range(1, near + 1):
+        arrived(h)
+        if h < reach:
+            pass_on(h + 1)
     gather_taps(head + 2, head + 4 + frames)
     active[pl.ds(2, frames)] = entry(head + 2, frames)
     time_copy.wait()
@@ -207,9 +236,10 @@
         if frames > skip:
             summed[skip * size :] = summed[skip * size :] + times(2, frames - skip, tap)
 
-    for d, o in offsets:
-        if d * frames > frames + 1:
-            arrived(d, o)
+    for h in range(near + 1, reach + 1):
+        arrived(h)
+        if h < reach:
+            pass_on(h + 1)
     gather_taps(head, head + 2)
     early = entry(head, 2)
     known = lax.broadcasted_iota(jnp.int32, (2, 1, 1), 0) + (tm * frames - 2) >= 0
@@ -249,8 +279,8 @@
             for g in range(2 * frames):
                 for r in range(own_rows):
                     part = y[g, r]
-                    low = part[:, :LANES]
-                    wide[0, g, 2 * r + p, pl.ds(q, cols, stride=2), :] = low
+                    first = part[:, :LANES]
+                    wide[0, g, 2 * r + p, pl.ds(q, cols, stride=2), :] = first
                     rest = jnp.concatenate(
                         [part[:, LANES:], jnp.zeros((cols, 2 * LANES - co), jnp.float32)], axis=1
                     )
@@ -260,11 +290,17 @@
             out_v[:, row, :, :LANES] = wide[0, :, row].astype(out_v.dtype)
             out_v[:, row, :, LANES:] = wide[1, :, row][:, :, : co - LANES].astype(out_v.dtype)
 
-    for d, o in offsets:
-
-        @pl.when(inside(d, o))
-        def _():
-            remote(d, o).wait_send()
+    for there, o in ((low, -1), (high, 1)):
+
+        @pl.when(there)
+        def _():
+            along_rows(o).wait_send()
+
+    for h in range(1, reach + 1):
+
+        @pl.when(later & (tm >= h - 1))
+        def _():
+            along_time(h).wait_send()
 
 
 def shards(tm_count, space_count, latent, w_in, b_in, gain_in, w_time, b_time, w_up, b_up):
@@ -298,8 +334,8 @@
             pltpu.VMEM((2, 2 * frames, 2 * rows, 2 * cols, LANES), f32),
             pltpu.SemaphoreType.DMA((7,)),
             pltpu.SemaphoreType.DMA((9,)),
-            pltpu.SemaphoreType.DMA(((reach + 1) * 3,)),
-            pltpu.SemaphoreType.DMA(((reach + 1) * 3,)),
+            pltpu.SemaphoreType.DMA((reach + 2,)),
+            pltpu.SemaphoreType.DMA((reach + 2,)),
         ],
         compiler_params=pltpu.CompilerParams(collective_id=0, has_side_effects=True, vmem_limit_bytes=VMEM_BYTES - 2 * frames * 2 * rows * 2 * cols * (-(-co // LANES) * LANES) * 2),
     )(

time: 10.4 us -> 10.2 us (0.981)
  the two profiles are of different devices: /device:TPU:1 before, /device:TPU:18 now
where the time goes in v3:
time: 10.2 us; the launch traced here: 10.1 us
  Pallas kernels  9.37 us (92%)
  local copies, waits for them, and re-layouts  0.71 us (7%)
    pallas_call x1, Pallas kernels, shards(): pl.pallas_call(functools.partial(kernel, (tm_count, space_count, reach, f...  9.37 us
    unnamed x1, local copies, waits for them, and re-layouts  0.71 us

profile of v3, /device:TPU:18, one launch (start us, length us, event | category | flops | bytes accessed | tf_op | source)
XLA Modules:
  0.0 10.1 jit_solution(2334998219289708480)
XLA Ops:
  0.0 9.4 %shard_map.82 = bf16[4,4,32,192]{3,2,1,0:T(8,128)(2,1)S(1)} custom-call(bf16[2,2,16,16]{3,2,1,0:T(8,128)(2,1)} %lat_hbm.1, bf16[3,3,3,16,384]{4,3,2,1,0:T(8,128)(2,1)} %w_in_hbm.1, f32[384]{0:T(512)} %b_in_hbm.1, f32[384]{0:T(512)} %gain_hbm.1, bf16[3,384,768]{2,1,0:T(8,128)(2,1)} %w_time_hbm.1, f32[768]{0:T(1024)} %b_time_hbm.1, ...), custom_call_target="tpu_custom_call" | custom-call | tf_op jit(solution)/shard_map/pallas_call | solution.py:314
  9.4 0.7 %copy.10 = bf16[4,4,32,192]{3,2,1,0:T(8,128)(2,1)} copy(bf16[4,4,32,192]{3,2,1,0:T(8,128)(2,1)S(1)} %shard_map.82) | data formatting | bytes 393216

commit v4 on v3

--- a/solution.py
+++ b/solution.py
@@ -56,19 +56,22 @@
     out_rows = rows + 2
     tm = lax.axis_index("tm")
     space = lax.axis_index("space")
+    direct = [(1, -1), (1, 1), (1, 0), (0, -1), (0, 1)]
     low, high = space > 0, space < space_count - 1
     later = tm < tm_count - 1
 
+    def inside(d, o):
+        t, s = tm + d, space + o
+        return (t >= 0) & (t < tm_count) & (s >= 0) & (s < space_count)
+
     barrier = pltpu.get_barrier_semaphore()
-    for there, target in (
-        (low, {"space": space - 1}),
-        (high, {"space": space + 1}),
-        (tm > 0, {"tm": tm - 1}),
-    ):
-
-        @pl.when(there)
-        def _():
-            pl.semaphore_signal(barrier, inc=1, device_id=target, device_id_type=MESH)
+    for d, o in direct:
+
+        @pl.when(inside(-d, -o))
+        def _():
+            pl.semaphore_signal(
+                barrier, inc=1, device_id={"tm": tm - d, "space": space - o}, device_id_type=MESH
+            )
 
     lat_copy = pltpu.make_async_copy(lat_hbm, lat_v, local_sem.at[0])
     lat_copy.start()
@@ -94,6 +97,10 @@
         def _():
             ext[reach, k] = jnp.zeros(ext.shape[2:], ext.dtype)
 
+        @pl.when(jnp.logical_not(there) & (tm > 0))
+        def _():
+            ext[reach - 1, k] = jnp.zeros(ext.shape[2:], ext.dtype)
+
     for h in range(1, reach + 1):
 
         @pl.when(tm < h)
@@ -108,17 +115,16 @@
     pieces.append(jnp.zeros((cols, LANES - frames * rows * zc), jnp.float32))
     ext[reach, halo] = jnp.concatenate(pieces, axis=1).astype(ext.dtype)
 
-    pl.semaphore_wait(
-        barrier, low.astype(jnp.int32) + high.astype(jnp.int32) + later.astype(jnp.int32)
-    )
-
-    def along_rows(o):
+    pl.semaphore_wait(barrier, sum(inside(d, o).astype(jnp.int32) for d, o in direct))
+
+    def straight(d, o):
+        slot = reach + 3 * d + o + 1
         return pltpu.make_async_remote_copy(
             src_ref=ext.at[reach, halo],
-            dst_ref=ext.at[reach, halo - o],
-            send_sem=send_sem.at[reach + (o + 1) // 2],
-            recv_sem=recv_sem.at[reach + (o + 1) // 2],
-            device_id={"space": space + o},
+            dst_ref=ext.at[reach - d, halo - o],
+            send_sem=send_sem.at[slot],
+            recv_sem=recv_sem.at[slot],
+            device_id={"tm": tm + d, "space": space + o},
             device_id_type=MESH,
         )
 
@@ -132,11 +138,11 @@
             device_id_type=MESH,
         )
 
-    for there, o in ((low, -1), (high, 1)):
-
-        @pl.when(there)
-        def _():
-            along_rows(o).start()
+    for d, o in direct:
+
+        @pl.when(inside(d, o))
+        def _():
+            straight(d, o).start()
 
     up_copy.wait()
     step = 16
@@ -157,23 +163,26 @@
                         place = pl.ds((2 * n + m) * ch, ch)
                         w_phase[p, q, pl.ds(at, step), place] = both.astype(w_phase.dtype)
 
-    for there, o in ((low, 1), (high, -1)):
-
-        @pl.when(there)
-        def _():
-            along_rows(o).wait_recv()
-
     def pass_on(h):
         @pl.when(later & (tm >= h - 1))
         def _():
             along_time(h).start()
 
+    def landed(d, o):
+        @pl.when(inside(-d, -o))
+        def _():
+            straight(d, o).wait_recv()
+
     def arrived(h):
-        @pl.when(tm >= h)
-        def _():
-            along_time(h).wait_recv()
-
-    pass_on(1)
+        if h == 1:
+            for o in (-1, 1, 0):
+                landed(1, o)
+        else:
+
+            @pl.when(tm >= h)
+            def _():
+                along_time(h).wait_recv()
+
     for copy in w_in_copies + small_copies:
         copy.wait()
 
@@ -221,6 +230,8 @@
         arrived(h)
         if h < reach:
             pass_on(h + 1)
+    landed(0, -1)
+    landed(0, 1)
     gather_taps(head + 2, head + 4 + frames)
     active[pl.ds(2, frames)] = entry(head + 2, frames)
     time_copy.wait()
@@ -290,13 +301,13 @@
             out_v[:, row, :, :LANES] = wide[0, :, row].astype(out_v.dtype)
             out_v[:, row, :, LANES:] = wide[1, :, row][:, :, : co - LANES].astype(out_v.dtype)
 
-    for there, o in ((low, -1), (high, 1)):
-
-        @pl.when(there)
-        def _():
-            along_rows(o).wait_send()
-
-    for h in range(1, reach + 1):
+    for d, o in direct:
+
+        @pl.when(inside(d, o))
+        def _():
+            straight(d, o).wait_send()
+
+    for h in range(2, reach + 1):
 
         @pl.when(later & (tm >= h - 1))
         def _():
@@ -334,8 +345,8 @@
             pltpu.VMEM((2, 2 * frames, 2 * rows, 2 * cols, LANES), f32),
             pltpu.SemaphoreType.DMA((7,)),
             pltpu.SemaphoreType.DMA((9,)),
-            pltpu.SemaphoreType.DMA((reach + 2,)),
-            pltpu.SemaphoreType.DMA((reach + 2,)),
+            pltpu.SemaphoreType.DMA((reach + 6,)),
+            pltpu.SemaphoreType.DMA((reach + 6,)),
         ],
         compiler_params=pltpu.CompilerParams(collective_id=0, has_side_effects=True, vmem_limit_bytes=VMEM_BYTES - 2 * frames * 2 * rows * 2 * cols * (-(-co // LANES) * LANES) * 2),
     )(

time: 10.2 us -> 9.4 us (0.922)
  the two profiles are of different devices: /device:TPU:18 before, /device:TPU:1 now
where the time goes in v4:
time: 9.4 us; the launch traced here: 9.26 us
  Pallas kernels  8.55 us (91%)
  local copies, waits for them, and re-layouts  0.71 us (8%)
    pallas_call x1, Pallas kernels, shards(): pl.pallas_call(functools.partial(kernel, (tm_count, space_count, reach, f...  8.55 us
    unnamed x1, local copies, waits for them, and re-layouts  0.71 us

profile of v4, /device:TPU:1, one launch (start us, length us, event | category | flops | bytes accessed | tf_op | source)
XLA Modules:
  0.0 9.3 jit_solution(11482054121184772026)
XLA Ops:
  0.0 8.5 %shard_map.82 = bf16[4,4,32,192]{3,2,1,0:T(8,128)(2,1)S(1)} custom-call(bf16[2,2,16,16]{3,2,1,0:T(8,128)(2,1)} %lat_hbm.1, bf16[3,3,3,16,384]{4,3,2,1,0:T(8,128)(2,1)} %w_in_hbm.1, f32[384]{0:T(512)} %b_in_hbm.1, f32[384]{0:T(512)} %gain_hbm.1, bf16[3,384,768]{2,1,0:T(8,128)(2,1)} %w_time_hbm.1, f32[768]{0:T(1024)} %b_time_hbm.1, ...), custom_call_target="tpu_custom_call" | custom-call | tf_op jit(solution)/shard_map/pallas_call | solution.py:325
  8.6 0.7 %copy.10 = bf16[4,4,32,192]{3,2,1,0:T(8,128)(2,1)} copy(bf16[4,4,32,192]{3,2,1,0:T(8,128)(2,1)S(1)} %shard_map.82) | data formatting | bytes 393216

commit v5 on v4

--- a/solution.py
+++ b/solution.py
@@ -35,6 +35,7 @@
     w_time_v,
     w_up_v,
     w_phase,
+    w_flat,
     b_in_v,
     gain_v,
     b_time_v,
@@ -168,6 +169,10 @@
         def _():
             along_time(h).start()
 
+    for p in range(2):
+        for q in range(2):
+            w_flat[p, q] = w_phase[p, q].T
+
     def landed(d, o):
         @pl.when(inside(-d, -o))
         def _():
@@ -282,9 +287,7 @@
                 ],
                 axis=1,
             )
-            y = lax.dot_general(
-                lhs, w_phase[p, q], (((1,), (1,)), ((), ())), preferred_element_type=jnp.float32
-            )
+            y = jnp.dot(lhs, w_flat[p, q], preferred_element_type=jnp.float32)
             y = y + b_up_v[...].reshape(1, co)
             y = y.reshape(2 * frames, own_rows, cols, co)
             for g in range(2 * frames):
@@ -335,6 +338,7 @@
             pltpu.VMEM(w_time.shape, bf16),
             pltpu.VMEM((3, 3, co, ch), bf16),
             pltpu.VMEM((2, 2, co, 4 * ch), bf16),
+            pltpu.VMEM((2, 2, 4 * ch, co), bf16),
             pltpu.VMEM((ch,), f32),
             pltpu.VMEM((ch,), f32),
             pltpu.VMEM((2 * ch,), f32),

time: 9.4 us -> 9.22 us (0.981)
  Pallas kernels: 8.55 us -> 8.36 us
    pallas_call x1, Pallas kernels: 8.55 us -> 8.36 us  [shards(): pl.pallas_call(functools.partial(kernel, (tm_count, space_count, reach, f...]
where the time goes in v5:
time: 9.22 us; the launch traced here: 9.08 us
  Pallas kernels  8.36 us (91%)
  local copies, waits for them, and re-layouts  0.71 us (8%)
    pallas_call x1, Pallas kernels, shards(): pl.pallas_call(functools.partial(kernel, (tm_count, space_count, reach, f...  8.36 us
    unnamed x1, local copies, waits for them, and re-layouts  0.71 us

profile of v5, /device:TPU:1, one launch (start us, length us, event | category | flops | bytes accessed | tf_op | source)
XLA Modules:
  0.0 9.1 jit_solution(2916934476615515618)
XLA Ops:
  0.0 8.4 %shard_map.82 = bf16[4,4,32,192]{3,2,1,0:T(8,128)(2,1)S(1)} custom-call(bf16[2,2,16,16]{3,2,1,0:T(8,128)(2,1)} %lat_hbm.1, bf16[3,3,3,16,384]{4,3,2,1,0:T(8,128)(2,1)} %w_in_hbm.1, f32[384]{0:T(512)} %b_in_hbm.1, f32[384]{0:T(512)} %gain_hbm.1, bf16[3,384,768]{2,1,0:T(8,128)(2,1)} %w_time_hbm.1, f32[768]{0:T(1024)} %b_time_hbm.1, ...), custom_call_target="tpu_custom_call" | custom-call | tf_op jit(solution)/shard_map/pallas_call | solution.py:328
  8.4 0.7 %copy.10 = bf16[4,4,32,192]{3,2,1,0:T(8,128)(2,1)} copy(bf16[4,4,32,192]{3,2,1,0:T(8,128)(2,1)S(1)} %shard_map.82) | data formatting | bytes 393216
